TPU v7x, 256 devices: a whole 4x4x8 slice. The times are simulated.
256 devices in a mesh: dp: 8 (over z_hi, core), expert: 32 (over x, z_lo, y).
Axes of the slice: x: 4, y: 4, z: 8 (z_hi: 4, z_lo: 2; z = z_hi * 2 + z_lo), core: 2. Of those that a mesh axis runs over, the one named last changes fastest.
Arguments:
- tokens: bfloat16 [256, 256, 1024], P(('dp', 'expert'))
- router: bfloat16 [1024, 128], replicated
- weight_in: bfloat16 [128, 1024, 2048], P('expert', None, 'dp'), may hold values from -0.1875 to 0.1875
- weight_out: bfloat16 [128, 2048, 1024], P('expert', 'dp'), may hold values from -0.125 to 0.125
- cotangent: bfloat16 [256, 256, 1024], P(('dp', 'expert')), may hold values from -6 to 6
Outputs:
- mixed: bfloat16 [256, 256, 1024], P(('dp', 'expert'))
- grad_tokens: bfloat16 [256, 256, 1024], P(('dp', 'expert'))
- grad_router: float32 [1024, 128], replicated
- grad_weight_in: bfloat16 [128, 1024, 2048], P('expert', None, 'dp')
- grad_weight_out: bfloat16 [128, 2048, 1024], P('expert', 'dp')
All inputs are finite; a program needn't handle non-finite values.
Results may differ from a plain program's by a relative error of at most 0.018.
Values may be sent and summed in bfloat16 or wider, within the bound.
A program may use at most 64 MiB of HBM per device.

v0:
```python
import jax
import jax.numpy as jnp
from jax import lax
from jax.sharding import PartitionSpec as P


def gelu_exact(values):
    return jax.nn.gelu(values, approximate=False)


def local(tokens, router, weight_in, weight_out, cotangent):
    experts_dev = weight_in.shape[0]
    width = tokens.shape[2]
    logits = jnp.einsum("isd,de->ise", tokens, router, preferred_element_type=jnp.float32)
    dispatch_prob = jax.nn.softmax(logits, axis=1)
    combine_prob = jax.nn.softmax(logits, axis=2)
    dispatch = dispatch_prob.astype(jnp.bfloat16)
    combine = combine_prob.astype(jnp.bfloat16)
    slots = jnp.einsum("ise,isd->ied", dispatch, tokens, preferred_element_type=jnp.float32).astype(
        jnp.bfloat16
    )
    grad_slots = jnp.einsum(
        "ise,isd->ied", combine, cotangent, preferred_element_type=jnp.float32
    ).astype(jnp.bfloat16)

    def to_owners(local_rows):
        arrived = lax.all_to_all(local_rows, "expert", split_axis=1, concat_axis=1, tiled=True)
        return lax.all_gather(arrived, "dp", axis=0, tiled=True)

    def from_owners(partial_value):
        summed = lax.psum_scatter(partial_value, "dp", scatter_dimension=0, tiled=True).astype(
            jnp.float32
        )
        return lax.all_to_all(
            summed.astype(jnp.bfloat16), "expert", split_axis=1, concat_axis=1, tiled=True
        )

    slot_rows = to_owners(slots)
    blocks = slot_rows.reshape(-1, experts_dev, width)
    pre_act = jnp.einsum("rkd,kdf->rkf", blocks, weight_in, preferred_element_type=jnp.float32)
    hidden = gelu_exact(pre_act).astype(jnp.bfloat16)
    partial_value = jnp.einsum(
        "rkf,kfd->rkd", hidden, weight_out, preferred_element_type=jnp.float32
    )
    blocks, pre_act, hidden, partial_value = (
        blocks,
        pre_act,
        hidden,
        partial_value.astype(jnp.bfloat16).reshape(slot_rows.shape),
    )
    expert_outs = from_owners(partial_value)
    grad_rows = to_owners(grad_slots)
    grad_blocks = grad_rows.reshape(blocks.shape)
    grad_hidden = jnp.einsum(
        "rkd,kfd->rkf", grad_blocks, weight_out, preferred_element_type=jnp.float32
    )
    _, gelu_back = jax.vjp(gelu_exact, pre_act)
    grad_pre = gelu_back(grad_hidden)[0].astype(jnp.bfloat16)
    grad_second = jnp.einsum(
        "rkf,rkd->kfd", hidden, grad_blocks, preferred_element_type=jnp.float32
    ).astype(jnp.bfloat16)
    grad_first = jnp.einsum(
        "rkd,rkf->kdf", blocks, grad_pre, preferred_element_type=jnp.float32
    ).astype(jnp.bfloat16)
    partial_back = jnp.einsum(
        "rkf,kdf->rkd", grad_pre, weight_in, preferred_element_type=jnp.float32
    )
    grad_first, grad_second, partial_back = (
        grad_first,
        grad_second,
        partial_back.astype(jnp.bfloat16).reshape(grad_rows.shape),
    )
    grad_slot_all = from_owners(partial_back)
    mixed = jnp.einsum(
        "ise,ied->isd", combine, expert_outs, preferred_element_type=jnp.float32
    ).astype(jnp.bfloat16)
    grad_comb = jnp.einsum(
        "isd,ied->ise", cotangent, expert_outs, preferred_element_type=jnp.float32
    )
    grad_disp = jnp.einsum(
        "isd,ied->ise", tokens, grad_slot_all, preferred_element_type=jnp.float32
    )
    part_disp = dispatch_prob * (
        grad_disp - jnp.sum(dispatch_prob * grad_disp, axis=1, keepdims=True)
    )
    part_comb = combine_prob * (
        grad_comb - jnp.sum(combine_prob * grad_comb, axis=2, keepdims=True)
    )
    grad_logits = (part_disp + part_comb).astype(jnp.bfloat16)
    grad_tokens = (
        jnp.einsum("ise,ied->isd", dispatch, grad_slot_all, preferred_element_type=jnp.float32)
        + jnp.einsum("ise,de->isd", grad_logits, router, preferred_element_type=jnp.float32)
    ).astype(jnp.bfloat16)
    router_term = jnp.einsum("isd,ise->de", tokens, grad_logits, preferred_element_type=jnp.float32)
    grad_router = lax.psum(router_term, ("dp", "expert"))
    return (mixed, grad_tokens, grad_router, grad_first, grad_second)


def solution(mesh):
    return jax.shard_map(
        local,
        mesh=mesh,
        in_specs=(
            P(("dp", "expert"), None, None),
            P(),
            P("expert", None, "dp"),
            P("expert", "dp", None),
            P(("dp", "expert"), None, None),
        ),
        out_specs=(
            P(("dp", "expert"), None, None),
            P(("dp", "expert"), None, None),
            P(),
            P("expert", None, "dp"),
            P("expert", "dp", None),
        ),
        check_vma=False,
    )
```

profile of v0, /device:TPU:2, one launch (start us, length us, event | category | flops | bytes accessed | tf_op | source)
XLA Modules:
  0.0 497.0 jit_solution(17294189357701382762)
XLA Ops:
  13.6 16.7 %all_to_all.20 = bf16[32,2,2048]{2,1,0:T(2,128)(2,1)S(1)} all-to-all(bf16[32,2,2048]{2,1,0:T(2,128)(2,1)S(1)} %reshape.119), channel_id=1, replica_groups=mesh['dp'=8,'expert'=32] {'expert'}, dimensions={0} | all-to-all | bytes 524288 | tf_op jit(solution)/shard_map/all_to_all | solution.py:27
  34.6 12.8 %all_to_all.21 = bf16[32,2,2048]{2,1,0:T(2,128)(2,1)S(1)} all-to-all(bf16[32,2,2048]{2,1,0:T(2,128)(2,1)S(1)} %reshape.123), channel_id=1, replica_groups=mesh['dp'=8,'expert'=32] {'expert'}, dimensions={0} | all-to-all | bytes 524288 | tf_op jit(solution)/shard_map/all_to_all | solution.py:27
  48.7 18.3 %all-gather.3.cloned.1.call-done = bf16[8,128,1024]{2,1,0:T(8,128)(2,1)} async-done(((bf16[1,128,1024]{2,1,0:T(8,128)(2,1)}), bf16[8,128,1024]{2,1,0:T(8,128)(2,1)}) %all-gather.3.cloned.1.call-update) | async-done | bytes 2097168 | tf_op jit(solution)/shard_map/all_gather | solution.py:28
  67.0 4.1 reshape.112
  71.1 4.3 copy.53
  75.4 5.3 %fusion.13 = (bf16[256,4,256]{2,0,1:T(8,128)(2,1)S(1)}, f32[4,256,256]{2,1,0:T(8,128)}) fusion(bf16[256,4,1024]{0,2,1:T(8,128)(2,1)} %copy.53, bf16[4,1024,256]{2,1,0:T(8,128)(2,1)S(1)} %copy-done), kind=kOutput, calls=%fused_computation.29 | convolution fusion | flops 553910272 | bytes 5767168 | tf_op jit(solution)/shard_map/rkd,kdf->rkf/dot_general | solution.py:40
  80.7 23.0 %all-gather.5.cloned.1.call-done = bf16[8,128,1024]{2,1,0:T(8,128)(2,1)} async-done(((bf16[1,128,1024]{2,1,0:T(8,128)(2,1)}), bf16[8,128,1024]{2,1,0:T(8,128)(2,1)}) %all-gather.5.cloned.1.call-update) | async-done | bytes 2097168 | tf_op jit(solution)/shard_map/all_gather | solution.py:28
  103.7 4.1 reshape.116
  107.8 5.7 %fusion.19 = bf16[256,4,256]{2,0,1:T(8,128)(2,1)S(1)} fusion(bf16[4,256,1024]{2,1,0:T(8,128)(2,1)} %param.8, bf16[256,4,1024]{2,1,0:T(4,128)(2,1)} %reshape.116, f32[4,256,256]{2,1,0:T(8,128)} %get-tuple-element.33), kind=kOutput, calls=%fused_computation.35 | convolution fusion | flops 555745280 | bytes 5767168 | tf_op jit(solution)/shard_map/rkd,kfd->rkf/dot_general | solution.py:54
  114.3 2.9 copy.49
  117.2 4.0 reshape.117
  121.5 2.3 convert_bitcast_fusion.1
  123.8 2.9 copy.44
  126.8 3.9 reshape.113
  130.7 31.9 %reduce-scatter.5.cloned.1.call-done = bf16[1,128,1024]{2,1,0:T(8,128)(2,1)} async-done(((bf16[8,128,1024]{2,1,0:T(8,128)(2,1)}), bf16[1,128,1024]{2,1,0:T(8,128)(2,1)}) %reduce-scatter.5.cloned.1.call-update) | async-done | bytes 262160 | tf_op jit(solution)/shard_map/reduce_scatter | solution.py:31
  164.8 3.1 reduce.15
  168.8 7.7 %all-to-all-start.3 = ((bf16[32,2,2048]{2,1,0:T(2,128)(2,1)}), bf16[32,2,2048]{2,1,0:T(2,128)(2,1)S(1)}, u32[]{:S(2)}, u32[]{:S(2)}) async-start(bf16[32,2,2048]{2,1,0:T(2,128)(2,1)} %reshape.125), calls=%async_computation.5 | async-start | bytes 524288 | tf_op jit(solution)/shard_map/all_to_all | solution.py:34
  176.5 4.5 convolution_convert_fusion
  181.0 28.3 %reduce-scatter.3.cloned.1.call-done = bf16[1,128,1024]{2,1,0:T(8,128)(2,1)} async-done(((bf16[8,128,1024]{2,1,0:T(8,128)(2,1)}), bf16[1,128,1024]{2,1,0:T(8,128)(2,1)}) %reduce-scatter.3.cloned.1.call-update) | async-done | bytes 262160 | tf_op jit(solution)/shard_map/reduce_scatter | solution.py:31
  210.7 2.9 reduce.13
  215.4 7.4 %all-to-all-start.1 = ((bf16[32,2,2048]{2,1,0:T(2,128)(2,1)}), bf16[32,2,2048]{2,1,0:T(2,128)(2,1)}, u32[]{:S(2)}, u32[]{:S(2)}) async-start(bf16[32,2,2048]{2,1,0:T(2,128)(2,1)} %reshape.121), calls=%async_computation.2 | async-start | bytes 524288 | tf_op jit(solution)/shard_map/all_to_all | solution.py:34
  223.1 3.6 convolution_convert_fusion.1
  230.8 2.8 reshape.122
  243.1 245.3 %all-reduce.2.cloned.1.call-done = f32[1024,128]{0,1:T(8,128)} async-done(((f32[1024,128]{0,1:T(8,128)}), f32[1024,128]{0,1:T(8,128)}) %all-reduce.2.cloned.1.call-update) | async-done | bytes 524304 | tf_op jit(solution)/shard_map/psum | solution.py:95
  (56 shorter events, 34.9 us)
Async XLA Ops:
  7.2 68.3 %copy-start = (bf16[4,1024,256]{2,1,0:T(8,128)(2,1)S(1)}, bf16[4,1024,256]{2,1,0:T(8,128)(2,1)}, u32[]{:S(2)}) copy-start(bf16[4,1024,256]{2,1,0:T(8,128)(2,1)} %param.7) | copy-start | bytes 6291460
  7.2 59.8 %all-gather.3.cloned.1.call-start = ((), (), s32[]{:S(2)}) async-start(), calls=%async_computation.6 | async-start | bytes 2359296 | tf_op jit(solution)/shard_map/all_gather | solution.py:28
  10.4 21.1 %copy-start.1 = (bf16[1,256,1024]{2,1,0:T(8,128)(2,1)S(1)}, bf16[1,256,1024]{2,1,0:T(8,128)(2,1)}, u32[]{:S(2)}) copy-start(bf16[1,256,1024]{2,1,0:T(8,128)(2,1)} %param.9) | copy-start | bytes 1572868
  31.4 72.2 %all-gather.5.cloned.1.call-start = ((), (), s32[]{:S(2)}) async-start(), calls=%async_computation.8 | async-start | bytes 2359296 | tf_op jit(solution)/shard_map/all_gather | solution.py:28
  48.5 114.1 %reduce-scatter.5.cloned.1.call-start = ((), (), s32[]{:S(2)}) async-start(), calls=%async_computation.9 | async-start | bytes 2359296 | tf_op jit(solution)/shard_map/reduce_scatter | solution.py:31
  121.2 88.1 %reduce-scatter.3.cloned.1.call-start = ((), (), s32[]{:S(2)}) async-start(), calls=%async_computation.7 | async-start | bytes 2359296 | tf_op jit(solution)/shard_map/reduce_scatter | solution.py:31
  168.8 46.6 %all-to-all-start.3 = ((bf16[32,2,2048]{2,1,0:T(2,128)(2,1)}), bf16[32,2,2048]{2,1,0:T(2,128)(2,1)S(1)}, u32[]{:S(2)}, u32[]{:S(2)}) async-start(bf16[32,2,2048]{2,1,0:T(2,128)(2,1)} %reshape.125), calls=%async_computation.5 | async-start | bytes 524288 | tf_op jit(solution)/shard_map/all_to_all | solution.py:34
  215.4 15.4 %all-to-all-start.1 = ((bf16[32,2,2048]{2,1,0:T(2,128)(2,1)}), bf16[32,2,2048]{2,1,0:T(2,128)(2,1)}, u32[]{:S(2)}, u32[]{:S(2)}) async-start(bf16[32,2,2048]{2,1,0:T(2,128)(2,1)} %reshape.121), calls=%async_computation.2 | async-start | bytes 524288 | tf_op jit(solution)/shard_map/all_to_all | solution.py:34
  222.8 265.6 %all-reduce.2.cloned.1.call-start = ((), (), s32[]{:S(2)}) async-start(), calls=%async_computation.10 | async-start | bytes 1048576 | tf_op jit(solution)/shard_map/psum | solution.py:95
  233.6 3.9 copy-start.2
  235.2 1.6 copy-start.4
  235.2 5.7 %copy-start.3 = (bf16[1024,128]{1,0:T(8,128)(2,1)S(1)}, bf16[1024,128]{1,0:T(8,128)(2,1)}, u32[]{:S(2)}) copy-start(bf16[1024,128]{1,0:T(8,128)(2,1)} %param.6) | copy-start | bytes 786436
  236.8 0.7 copy-start.5
  236.8 0.7 copy-start.6
  236.8 0.6 copy-start.7
Sparse Core Ops, SparseCore 0:
  31.6 35.4 all-gather.2
  69.5 34.1 all-gather.4
  121.4 41.2 reduce-scatter.4
  165.6 43.6 reduce-scatter.2
  238.8 249.5 all-reduce.1
where the time goes:
time: 498 us; the launch traced here: 497 us
  waiting for transfers between devices  349 us (70%)
  local copies, waits for them, and re-layouts  42.7 us (9%)
  matrix products  35.6 us (7%)
  blocking collectives  29.5 us (6%)
  starting transfers between devices  16 us (3%)
  between operations  14 us (3%)
  other arithmetic  10.5 us (2%)
    psum x1, waiting for transfers between devices, local(): grad_router = lax.psum(router_term, ('dp', 'expert'))  245 us
    reduce_scatter x2, waiting for transfers between devices, from_owners(): lax.psum_scatter(partial_value, 'dp', scatter_dimension=0, tiled=True)  60.2 us
    all_gather x2, waiting for transfers between devices, to_owners(): return lax.all_gather(arrived, 'dp', axis=0, tiled=True)  41.3 us
    all_to_all x2, blocking collectives, to_owners(): lax.all_to_all(local_rows, 'expert', split_axis=1, concat_axis=1, tiled=T...  29.5 us
    all_to_all x2, starting transfers between devices, from_owners(): lax.all_to_all(summed.astype(jnp.bfloat16), 'expert', split_axis=1, conca...  15.1 us
    unnamed x26, local copies, waits for them, and re-layouts  10.5 us
    unnamed x4, other arithmetic  10.3 us
  transfers between devices with their start and end apart: 7, of which 6 were waited for; matrix products, arithmetic and copies ran while one was open for 11% of the time, Pallas kernels for 0%

commit v1 on v0

--- a/solution.py
+++ b/solution.py
@@ -92,7 +92,7 @@
         + jnp.einsum("ise,de->isd", grad_logits, router, preferred_element_type=jnp.float32)
     ).astype(jnp.bfloat16)
     router_term = jnp.einsum("isd,ise->de", tokens, grad_logits, preferred_element_type=jnp.float32)
-    grad_router = lax.psum(router_term, ("dp", "expert"))
+    grad_router = lax.psum(lax.psum(router_term, "dp"), "expert")
     return (mixed, grad_tokens, grad_router, grad_first, grad_second)
 
 

time: 498 us -> 616 us (1.24); the launches traced: 497 us -> 606 us
  waiting for transfers between devices: 349 us -> 459 us
    psum x1 -> x2, waiting for transfers between devices: 245 us -> 363 us  [local(): grad_router = lax.psum(lax.psum(router_term, 'dp'), 'expert')]
    all_gather x2, waiting for transfers between devices: 41.3 us -> 33.4 us  [to_owners(): return lax.all_gather(arrived, 'dp', axis=0, tiled=True)]
  transfers between devices with their start and end apart: 7 -> 8, of which waited for: 6 -> 7; matrix products, arithmetic and copies ran while one was open for 11% -> 12% of each run, Pallas kernels for 0% -> 0%
where the time goes in v1:
time: 616 us; the launch traced here: 606 us
  waiting for transfers between devices  459 us (75%)
  local copies, waits for them, and re-layouts  43.5 us (7%)
  matrix products  31.6 us (5%)
  blocking collectives  29.5 us (5%)
  starting transfers between devices  16.4 us (3%)
  between operations  14.3 us (2%)
  other arithmetic  11.6 us (2%)
    psum x2, waiting for transfers between devices, local(): grad_router = lax.psum(lax.psum(router_term, 'dp'), 'expert')  363 us
    reduce_scatter x2, waiting for transfers between devices, from_owners(): lax.psum_scatter(partial_value, 'dp', scatter_dimension=0, tiled=True)  58.2 us
    all_gather x2, waiting for transfers between devices, to_owners(): return lax.all_gather(arrived, 'dp', axis=0, tiled=True)  33.4 us
    all_to_all x2, blocking collectives, to_owners(): lax.all_to_all(local_rows, 'expert', split_axis=1, concat_axis=1, tiled=T...  29.5 us
    all_to_all x2, starting transfers between devices, from_owners(): lax.all_to_all(summed.astype(jnp.bfloat16), 'expert', split_axis=1, conca...  15.5 us
  transfers between devices with their start and end apart: 8, of which 7 were waited for; matrix products, arithmetic and copies ran while one was open for 12% of the time, Pallas kernels for 0%

profile of v1, /device:TPU:2, one launch (start us, length us, event | category | flops | bytes accessed | tf_op | source)
XLA Modules:
  0.0 606.4 jit_solution(9297212298693709992)
XLA Ops:
  13.7 16.7 %all_to_all.20 = bf16[32,2,2048]{2,1,0:T(2,128)(2,1)S(1)} all-to-all(bf16[32,2,2048]{2,1,0:T(2,128)(2,1)S(1)} %reshape.119), channel_id=1, replica_groups=mesh['dp'=8,'expert'=32] {'expert'}, dimensions={0} | all-to-all | bytes 524288 | tf_op jit(solution)/shard_map/all_to_all | solution.py:27
  34.8 12.8 %all_to_all.21 = bf16[32,2,2048]{2,1,0:T(2,128)(2,1)S(1)} all-to-all(bf16[32,2,2048]{2,1,0:T(2,128)(2,1)S(1)} %reshape.123), channel_id=1, replica_groups=mesh['dp'=8,'expert'=32] {'expert'}, dimensions={0} | all-to-all | bytes 524288 | tf_op jit(solution)/shard_map/all_to_all | solution.py:27
  48.8 18.3 %all-gather.3.cloned.1.call-done = bf16[8,128,1024]{2,1,0:T(8,128)(2,1)} async-done(((bf16[1,128,1024]{2,1,0:T(8,128)(2,1)}), bf16[8,128,1024]{2,1,0:T(8,128)(2,1)}) %all-gather.3.cloned.1.call-update) | async-done | bytes 2097168 | tf_op jit(solution)/shard_map/all_gather | solution.py:28
  67.1 4.1 reshape.112
  71.2 4.3 copy.53
  75.5 5.5 fusion.13
  81.7 2.9 copy.44
  84.7 4.0 reshape.113
  88.9 15.1 %all-gather.5.cloned.1.call-done = bf16[8,128,1024]{2,1,0:T(8,128)(2,1)} async-done(((bf16[1,128,1024]{2,1,0:T(8,128)(2,1)}), bf16[8,128,1024]{2,1,0:T(8,128)(2,1)}) %all-gather.5.cloned.1.call-update) | async-done | bytes 2097168 | tf_op jit(solution)/shard_map/all_gather | solution.py:28
  104.0 4.1 reshape.116
  108.1 5.7 fusion.19
  114.6 2.9 copy.49
  117.6 4.0 reshape.117
  121.5 26.2 %reduce-scatter.3.cloned.1.call-done = bf16[1,128,1024]{2,1,0:T(8,128)(2,1)} async-done(((bf16[8,128,1024]{2,1,0:T(8,128)(2,1)}), bf16[1,128,1024]{2,1,0:T(8,128)(2,1)}) %reduce-scatter.3.cloned.1.call-update) | async-done | bytes 262160 | tf_op jit(solution)/shard_map/reduce_scatter | solution.py:31
  149.9 3.2 reduce.13
  153.9 7.3 %all-to-all-start.1 = ((bf16[32,2,2048]{2,1,0:T(2,128)(2,1)}), bf16[32,2,2048]{2,1,0:T(2,128)(2,1)S(1)}, u32[]{:S(2)}, u32[]{:S(2)}) async-start(bf16[32,2,2048]{2,1,0:T(2,128)(2,1)} %reshape.121), calls=%async_computation.2 | async-start | bytes 524288 | tf_op jit(solution)/shard_map/all_to_all | solution.py:34
  161.3 32.0 %reduce-scatter.5.cloned.1.call-done = bf16[1,128,1024]{2,1,0:T(8,128)(2,1)} async-done(((bf16[8,128,1024]{2,1,0:T(8,128)(2,1)}), bf16[1,128,1024]{2,1,0:T(8,128)(2,1)}) %reduce-scatter.5.cloned.1.call-update) | async-done | bytes 262160 | tf_op jit(solution)/shard_map/reduce_scatter | solution.py:31
  195.4 3.9 reduce.15
  201.1 8.2 %all-to-all-start.3 = ((bf16[32,2,2048]{2,1,0:T(2,128)(2,1)}), bf16[32,2,2048]{2,1,0:T(2,128)(2,1)}, u32[]{:S(2)}, u32[]{:S(2)}) async-start(bf16[32,2,2048]{2,1,0:T(2,128)(2,1)} %reshape.125), calls=%async_computation.5 | async-start | bytes 524288 | tf_op jit(solution)/shard_map/all_to_all | solution.py:34
  212.1 5.2 all-to-all-done.3
  217.3 2.8 reshape.126
  224.5 4.6 convolution_convert_fusion
  231.2 62.8 %all-reduce.3.cloned.1.call-done = f32[1024,128]{0,1:T(8,128)} async-done(((f32[1024,128]{0,1:T(8,128)}), f32[1024,128]{0,1:T(8,128)}) %all-reduce.3.cloned.1.call-update) | async-done | bytes 524304 | tf_op jit(solution)/shard_map/psum | solution.py:95
  297.8 299.7 %all-reduce.5.cloned.1.call-done = f32[1024,128]{0,1:T(8,128)} async-done(((f32[1024,128]{0,1:T(8,128)}), f32[1024,128]{0,1:T(8,128)}) %all-reduce.5.cloned.1.call-update) | async-done | bytes 524304 | tf_op jit(solution)/shard_map/psum | solution.py:95
  (63 shorter events, 35.8 us)
Async XLA Ops:
  7.2 68.3 %copy-start = (bf16[4,1024,256]{2,1,0:T(8,128)(2,1)S(1)}, bf16[4,1024,256]{2,1,0:T(8,128)(2,1)}, u32[]{:S(2)}) copy-start(bf16[4,1024,256]{2,1,0:T(8,128)(2,1)} %param.7) | copy-start | bytes 6291460
  7.2 59.9 %all-gather.3.cloned.1.call-start = ((), (), s32[]{:S(2)}) async-start(), calls=%async_computation.6 | async-start | bytes 2359296 | tf_op jit(solution)/shard_map/all_gather | solution.py:28
  10.4 21.2 %copy-start.2 = (bf16[1,256,1024]{2,1,0:T(8,128)(2,1)S(1)}, bf16[1,256,1024]{2,1,0:T(8,128)(2,1)}, u32[]{:S(2)}) copy-start(bf16[1,256,1024]{2,1,0:T(8,128)(2,1)} %param.9) | copy-start | bytes 1572868
  31.5 72.5 %all-gather.5.cloned.1.call-start = ((), (), s32[]{:S(2)}) async-start(), calls=%async_computation.8 | async-start | bytes 2359296 | tf_op jit(solution)/shard_map/all_gather | solution.py:28
  48.6 99.2 %reduce-scatter.3.cloned.1.call-start = ((), (), s32[]{:S(2)}) async-start(), calls=%async_computation.7 | async-start | bytes 2359296 | tf_op jit(solution)/shard_map/reduce_scatter | solution.py:31
  75.5 5.5 copy-start.4
  88.7 104.6 %reduce-scatter.5.cloned.1.call-start = ((), (), s32[]{:S(2)}) async-start(), calls=%async_computation.9 | async-start | bytes 2359296 | tf_op jit(solution)/shard_map/reduce_scatter | solution.py:31
  153.9 47.1 %all-to-all-start.1 = ((bf16[32,2,2048]{2,1,0:T(2,128)(2,1)}), bf16[32,2,2048]{2,1,0:T(2,128)(2,1)S(1)}, u32[]{:S(2)}, u32[]{:S(2)}) async-start(bf16[32,2,2048]{2,1,0:T(2,128)(2,1)} %reshape.121), calls=%async_computation.2 | async-start | bytes 524288 | tf_op jit(solution)/shard_map/all_to_all | solution.py:34
  201.1 16.2 %all-to-all-start.3 = ((bf16[32,2,2048]{2,1,0:T(2,128)(2,1)}), bf16[32,2,2048]{2,1,0:T(2,128)(2,1)}, u32[]{:S(2)}, u32[]{:S(2)}) async-start(bf16[32,2,2048]{2,1,0:T(2,128)(2,1)} %reshape.125), calls=%async_computation.5 | async-start | bytes 524288 | tf_op jit(solution)/shard_map/all_to_all | solution.py:34
  209.3 84.8 %all-reduce.3.cloned.1.call-start = ((), (), s32[]{:S(2)}) async-start(), calls=%async_computation.10 | async-start | bytes 1048576 | tf_op jit(solution)/shard_map/psum | solution.py:95
  221.6 0.6 copy-start.6
  221.6 0.6 copy-start.8
  224.5 373.1 %all-reduce.5.cloned.1.call-start = ((), (), s32[]{:S(2)}) async-start(), calls=%async_computation.11 | async-start | bytes 1048576 | tf_op jit(solution)/shard_map/psum | solution.py:95
  224.5 4.7 copy-start.1
  229.2 64.9 %copy-start.3 = (bf16[128,1,1024]{2,1,0:T(2,128)(2,1)S(1)}, bf16[128,1,1024]{2,1,0:T(2,128)(2,1)}, u32[]{:S(2)}) copy-start(bf16[128,1,1024]{2,1,0:T(2,128)(2,1)} %reshape.122) | copy-start | bytes 786436
  231.2 65.4 %copy-start.5 = (bf16[1024,128]{1,0:T(8,128)(2,1)S(1)}, bf16[1024,128]{1,0:T(8,128)(2,1)}, u32[]{:S(2)}) copy-start(bf16[1024,128]{1,0:T(8,128)(2,1)} %param.6) | copy-start | bytes 786436
  231.2 65.4 %copy-start.7 = (f32[256]{0:T(256)S(1)}, f32[256]{0:T(256)}, u32[]{:S(2)}) copy-start(f32[256]{0:T(256)} %copy-done.6) | copy-start | bytes 3076
  231.2 65.4 %copy-start.9 = (f32[128]{0:T(128)S(1)}, f32[128]{0:T(128)}, u32[]{:S(2)}) copy-start(f32[128]{0:T(128)} %copy-done.8) | copy-start | bytes 1540
Sparse Core Ops, SparseCore 0:
  31.7 35.4 all-gather.2
  69.6 34.4 all-gather.4
  106.6 41.1 reduce-scatter.2
  150.2 43.0 reduce-scatter.4
  224.6 69.4 all-reduce.2
  296.7 300.7 all-reduce.4
